TPU v7x, 32 devices: a whole 2x2x4 slice. The times are simulated.
32 devices in a mesh: tok: 8 (over y, x, core), mdl: 4 (over z).
Axes of the slice: x: 2, y: 2, z: 4, core: 2. Of those that a mesh axis runs over, the one named last changes fastest.
Arguments:
- hidden_states: bfloat16 [4096, 3072], P('tok', 'mdl'), may hold values from -36 to 36
- lengths: int32 [2], replicated, may hold values from 1 to 2277, 3644 in all
- positions: int32 [3, 4096], P(None, 'tok'), may hold values from 0 to 44, as said below
- modulation: float32 [6, 3072], replicated, may hold values from -3 to 3
- query_weight: bfloat16 [3072, 3072], P('tok', 'mdl'), may hold values from -1.1 to 1.1
- key_weight: bfloat16 [3072, 3072], P('tok', 'mdl'), may hold values from -1.1 to 1.1
- value_weight: bfloat16 [3072, 3072], P('tok', 'mdl'), may hold values from -0.109375 to 0.109375
- out_weight: bfloat16 [3072, 3072], P('tok', 'mdl'), may hold values from -0.109375 to 0.109375
- query_gain: float32 [64], replicated, may hold values from 0.1 to 1.9
- key_gain: float32 [64], replicated, may hold values from 0.1 to 1.9
Outputs:
- updated: bfloat16 [4096, 3072], P('tok', 'mdl')
Inputs may be any that keep to these rules, and one draw needn't show every extreme that they name: lengths[0] + lengths[1] = 3644, and neither of them exceeds 2277. `positions`: frame below 13, row below 30, column below 45.
All inputs are finite; a program needn't handle non-finite values.
Results may differ from a plain program's by a relative error of at most 0.0045.
Values may be sent and summed in bfloat16 or wider, within the bound.
A program may use at most 128 MiB of HBM per device.

v0:
```python
import jax
import jax.numpy as jnp
from jax import lax
from jax.sharding import PartitionSpec as P

TEXT = 226


def token_labels(row_index, lengths):
    bound = TEXT + lengths[0]
    request = (row_index >= bound).astype(jnp.int32)
    place = row_index - request * bound
    return (request, place < TEXT, bound)


def modulate(rows_bf, modulation, is_text):
    values = rows_bf.astype(jnp.float32)
    center = values - jnp.mean(values, axis=1, keepdims=True)
    spread = jnp.mean(center * center, axis=1, keepdims=True)
    normal = center * lax.rsqrt(spread + 1e-05)
    textual = is_text[:, None]
    shift = jnp.where(textual, modulation[3][None, :], modulation[0][None, :])
    scale = jnp.where(textual, modulation[4][None, :], modulation[1][None, :])
    return (normal * (1.0 + scale) + shift).astype(jnp.bfloat16)


def pair_angles(positions, pairs):
    index = jnp.arange(pairs, dtype=jnp.int32)
    first = pairs // 4
    second = (pairs - first) // 2
    third = pairs - first - second
    component = jnp.where(index < first, 0, jnp.where(index < first + second, 1, 2))
    local = index - jnp.where(component == 0, 0, jnp.where(component == 1, first, first + second))
    count = jnp.where(component == 0, first, jnp.where(component == 1, second, third))
    rates = jnp.power(jnp.float32(10000.0), -local.astype(jnp.float32) / count.astype(jnp.float32))
    places = positions.astype(jnp.float32)
    chosen = jnp.where(
        component[:, None] == 0,
        places[0][None, :],
        jnp.where(component[:, None] == 1, places[1][None, :], places[2][None, :]),
    )
    return jnp.transpose(chosen * rates[:, None])


def head_norm(projected, gain, angles, is_text):
    width = gain.shape[0]
    shaped = projected.reshape(projected.shape[0], -1, width)
    center = shaped - jnp.mean(shaped, axis=2, keepdims=True)
    spread = jnp.mean(center * center, axis=2, keepdims=True)
    normal = center * lax.rsqrt(spread + 1e-06) * gain
    half = width // 2
    cosine = jnp.cos(angles)[:, None, :]
    sine = jnp.sin(angles)[:, None, :]
    lower = normal[:, :, :half]
    upper = normal[:, :, half:]
    turned = jnp.concatenate([lower * cosine - upper * sine, lower * sine + upper * cosine], axis=2)
    return jnp.where(is_text[:, None, None], normal, turned).astype(jnp.bfloat16)


def shards(
    hidden_states,
    lengths,
    positions,
    modulation,
    query_weight,
    key_weight,
    value_weight,
    out_weight,
    query_gain,
    key_gain,
):
    own_rows = hidden_states.shape[0]
    local_width = query_weight.shape[1]
    head_width = query_gain.shape[0]
    local_heads = local_width // head_width
    full_rows = lax.all_gather(hidden_states, "mdl", axis=1, tiled=True)
    row_index = lax.axis_index("tok") * own_rows + jnp.arange(own_rows, dtype=jnp.int32)
    request, is_text, bound = token_labels(row_index, lengths)
    normed = modulate(full_rows, modulation, is_text)
    angles = pair_angles(positions, head_width // 2)
    pieces = (
        lax.all_gather(query_weight, "tok", axis=0, tiled=True),
        lax.all_gather(key_weight, "tok", axis=0, tiled=True),
        lax.all_gather(value_weight, "tok", axis=0, tiled=True),
    )
    columns = normed
    query_sum, key_sum, value_sum = tuple(
        (
            jnp.dot(columns, pieces[number], preferred_element_type=jnp.float32)
            for number in range(3)
        )
    )
    query = head_norm(query_sum, query_gain, angles, is_text)
    key_flat = head_norm(key_sum, key_gain, angles, is_text).reshape(own_rows, local_width)
    value_flat = value_sum.astype(jnp.bfloat16)
    factor = head_width ** (-0.5)

    def block_terms(block_keys, block_values, block_start):
        size = block_keys.shape[0]
        key_request = (block_start + jnp.arange(size, dtype=jnp.int32) >= bound).astype(jnp.int32)
        score = (
            jnp.einsum(
                "qhd,khd->hqk",
                query,
                block_keys.reshape(size, local_heads, head_width),
                preferred_element_type=jnp.float32,
            )
            * factor
        )
        same = (request[:, None] == key_request[None, :])[None, :, :]
        expo = jnp.where(same, jnp.exp(score), jnp.float32(0.0))
        totals = jnp.transpose(jnp.sum(expo, axis=2))
        weighted = jnp.einsum(
            "hqk,khd->qhd",
            expo.astype(jnp.bfloat16),
            block_values.reshape(size, local_heads, head_width),
            preferred_element_type=jnp.float32,
        )
        return (weighted.reshape(own_rows, local_width), totals)

    initial = (
        jnp.zeros((own_rows, local_width), jnp.float32),
        jnp.zeros((own_rows, local_heads), jnp.float32),
    )
    keys_piece = lax.all_gather(key_flat, "tok", axis=0, tiled=True)
    values_piece = lax.all_gather(value_flat, "tok", axis=0, tiled=True)
    count = keys_piece.shape[0]
    block = 1024
    steps_count = count // block

    def step_block(inner, operands):
        block_keys, block_values, offset = operands
        weighted, totals = block_terms(block_keys, block_values, offset)
        return ((inner[0] + weighted, inner[1] + totals), None)

    offsets = jnp.arange(steps_count, dtype=jnp.int32) * block
    result, unused = lax.scan(
        step_block,
        initial,
        (
            keys_piece.reshape(steps_count, block, local_width),
            values_piece.reshape(steps_count, block, local_width),
            offsets,
        ),
    )
    weighted, totals = result
    attended = (
        (weighted.reshape(own_rows, local_heads, head_width) / totals[:, :, None])
        .reshape(own_rows, local_width)
        .astype(jnp.bfloat16)
    )
    all_heads = lax.all_gather(attended, "mdl", axis=1, tiled=True)
    out_width = out_weight.shape[1]
    columns = all_heads
    projected = jnp.dot(
        columns,
        lax.all_gather(out_weight, "tok", axis=0, tiled=True),
        preferred_element_type=jnp.float32,
    )
    gate_rows = lax.dynamic_slice_in_dim(
        modulation, lax.axis_index("mdl") * out_width, out_width, 1
    )
    gate = jnp.where(is_text[:, None], gate_rows[5][None, :], gate_rows[2][None, :])
    return (hidden_states.astype(jnp.float32) + gate * projected).astype(jnp.bfloat16)


def solution(mesh):
    return jax.shard_map(
        shards,
        mesh=mesh,
        in_specs=(
            P("tok", "mdl"),
            P(),
            P(None, "tok"),
            P(),
            P("tok", "mdl"),
            P("tok", "mdl"),
            P("tok", "mdl"),
            P("tok", "mdl"),
            P(),
            P(),
        ),
        out_specs=P("tok", "mdl"),
        check_vma=False,
    )
```

profile of v0, /device:TPU:0, one launch (start us, length us, event | category | flops | bytes accessed | tf_op | source)
XLA Modules:
  0.0 505.0 jit_solution(1737966056882740450)
XLA Ops:
  6.6 0.7 all-gather.9.cloned.1.call-update
  7.3 0.7 all-gather.15.cloned.1.call-update
  8.1 0.7 all-gather.19.cloned.1.call-update
  9.6 1.0 fusion.20
  10.6 64.5 %all-gather.9.cloned.1.call-done = bf16[512,3072]{1,0:T(8,128)(2,1)} async-done(((bf16[512,768]{1,0:T(8,128)(2,1)}), bf16[512,3072]{1,0:T(8,128)(2,1)}) %all-gather.9.cloned.1.call-update) | async-done | bytes 3145744 | tf_op jit(solution)/shard_map/all_gather | solution.py:76
  75.1 2.5 convert_reduce_fusion
  78.0 1.0 fusion.13
  78.9 3.7 fusion.16
  82.7 32.0 %all-gather.15.cloned.1.call-done = bf16[3072,768]{1,0:T(8,128)(2,1)} async-done(((bf16[384,768]{1,0:T(8,128)(2,1)}), bf16[3072,768]{1,0:T(8,128)(2,1)}) %all-gather.15.cloned.1.call-update) | async-done | bytes 4718608 | tf_op jit(solution)/shard_map/all_gather | solution.py:83
  114.7 5.9 %fusion.25 = f32[512,768]{1,0:T(8,128)S(1)} fusion(bf16[512,3072]{1,0:T(8,128)(2,1)} %fusion.16, bf16[3072,768]{1,0:T(8,128)(2,1)} %all-gather.15.cloned.1.call-done), kind=kOutput, calls=%fused_computation.64 | convolution fusion | flops 2415919104 | bytes 9437184 | tf_op jit(solution)/shard_map/dot_general | solution.py:89
  121.0 0.7 copy-done.3
  121.9 33.6 %all-gather.19.cloned.1.call-done = bf16[3072,768]{1,0:T(8,128)(2,1)} async-done(((bf16[384,768]{1,0:T(8,128)(2,1)}), bf16[3072,768]{1,0:T(8,128)(2,1)}) %all-gather.19.cloned.1.call-update) | async-done | bytes 4718608 | tf_op jit(solution)/shard_map/all_gather | solution.py:82
  155.5 5.5 %fusion.26 = f32[512,768]{0,1:T(8,128)S(1)} fusion(bf16[512,3072]{1,0:T(8,128)(2,1)} %fusion.16, bf16[3072,768]{1,0:T(8,128)(2,1)} %all-gather.19.cloned.1.call-done), kind=kOutput, calls=%fused_computation.65 | convolution fusion | flops 2415919104 | bytes 9437184 | tf_op jit(solution)/shard_map/dot_general | solution.py:89
  163.4 1.3 multiply_subtract_fusion
  164.8 1.2 copy.23
  165.9 0.9 mul.163
  166.9 1.7 copy.22
  168.5 0.9 sub.56
  169.5 1.6 copy.21
  171.1 3.8 select_convert_fusion
  175.1 21.0 %all-gather.11.cloned.1.call-done = bf16[3072,768]{1,0:T(8,128)(2,1)} async-done(((bf16[384,768]{1,0:T(8,128)(2,1)}), bf16[3072,768]{1,0:T(8,128)(2,1)}) %all-gather.11.cloned.1.call-update) | async-done | bytes 4718608 | tf_op jit(solution)/shard_map/all_gather | solution.py:84
  196.2 6.8 %convolution_convert_fusion = bf16[512,768]{1,0:T(8,128)(2,1)} fusion(bf16[512,3072]{1,0:T(8,128)(2,1)} %fusion.16, bf16[3072,768]{1,0:T(8,128)(2,1)} %all-gather.11.cloned.1.call-done), kind=kOutput, calls=%fused_computation.36 | convolution fusion | flops 2416312320 | bytes 8650752 | tf_op jit(solution)/shard_map/dot_general | solution.py:89
  203.0 0.7 all-gather.23.cloned.1.call-update
  204.0 1.3 fusion.17
  205.3 38.2 %all-gather.17.cloned.1.call-done = bf16[4096,768]{1,0:T(8,128)(2,1)} async-done(((bf16[512,768]{1,0:T(8,128)(2,1)}), bf16[4096,768]{1,0:T(8,128)(2,1)}) %all-gather.17.cloned.1.call-update) | async-done | bytes 6291472 | tf_op jit(solution)/shard_map/all_gather | solution.py:125
  243.5 47.3 %all-gather.13.cloned.1.call-done = bf16[4096,768]{1,0:T(8,128)(2,1)} async-done(((bf16[512,768]{1,0:T(8,128)(2,1)}), bf16[4096,768]{1,0:T(8,128)(2,1)}) %all-gather.13.cloned.1.call-update) | async-done | bytes 6291472 | tf_op jit(solution)/shard_map/all_gather | solution.py:126
  290.8 134.3 %while.15 = (s32[]{:T(128)}, f32[512,768]{0,1:T(8,128)}, f32[512,12]{0,1:T(8,128)}, bf16[4,1024,768]{2,1,0:T(8,128)(2,1)}, s32[4]{0:T(128)S(1)}, /*index=5*/s32[...) while((s32[]{:T(128)}, f32[512,768]{0,1:T(8,128)}, ...), condition=%wide.region_8.9_spmd.clone.clone.clone, body=%wide.region_6.8_spmd.clone.clone.clone.sunk | while | flops 1649682944 | bytes 87601416 | solution.py:137
  290.8 0.6 dynamic_slice.29
  291.4 0.6 fusion.51
  292.0 1.2 broadcast_compare_fusion.4
  293.2 2.1 constant_dynamic-slice_fusion.3
  295.3 1.6 copy.34
  296.9 13.0 %fusion.52 = (f32[12,512]{1,0:T(8,128)S(1)}, f32[12,1024,512]{2,1,0:T(8,128)}) fusion(pred[512,1024]{0,1:T(8,128)(4,1)} %broadcast_compare_fusion.4, bf16[1024,12,64]{0,2,1:T(8,128)(2,1)} %bitcast.67, bf16[512,12,64]{0,2,1:T(8,128)(2,1)} %get-tuple-element.289), kind=kOutput, calls=%fused_computation.2.clone.1 | convolution fusion | flops 824174592 | bytes 28073984 | tf_op jit(solution)/shard_map/while/body/eval_jaxpr/qhd,khd->hqk/dot_general | solution.py:102
  309.9 1.6 copy.33
  311.5 11.7 %fusion.53 = f32[12,64,512]{2,1,0:T(8,128)S(1)} fusion(bf16[1024,12,64]{0,2,1:T(8,128)(2,1)} %bitcast.68, f32[12,1024,512]{2,1,0:T(8,128)} %get-tuple-element.258, pred[512,1024]{0,1:T(8,128)(4,1)} %broadcast_compare_fusion.4), kind=kOutput, calls=%fused_computation.4.clone.1 | convolution fusion | flops 824180736 | bytes 28835840 | tf_op jit(solution)/shard_map/while/body/eval_jaxpr/hqk,khd->qhd/dot_general | solution.py:113
  324.0 0.9 copy-done.1
  325.5 0.6 fusion.51
  326.2 1.2 broadcast_compare_fusion.4
  327.3 2.1 constant_dynamic-slice_fusion.3
  329.5 1.6 copy.34
  331.1 13.0 %fusion.52 = (f32[12,512]{1,0:T(8,128)S(1)}, f32[12,1024,512]{2,1,0:T(8,128)}) fusion(pred[512,1024]{0,1:T(8,128)(4,1)} %broadcast_compare_fusion.4, bf16[1024,12,64]{0,2,1:T(8,128)(2,1)} %bitcast.67, bf16[512,12,64]{0,2,1:T(8,128)(2,1)} %get-tuple-element.289), kind=kOutput, calls=%fused_computation.2.clone.1 | convolution fusion | flops 824174592 | bytes 28073984 | tf_op jit(solution)/shard_map/while/body/eval_jaxpr/qhd,khd->hqk/dot_general | solution.py:102
  344.1 1.6 copy.33
  345.7 10.9 %fusion.53 = f32[12,64,512]{2,1,0:T(8,128)S(1)} fusion(bf16[1024,12,64]{0,2,1:T(8,128)(2,1)} %bitcast.68, f32[12,1024,512]{2,1,0:T(8,128)} %get-tuple-element.258, pred[512,1024]{0,1:T(8,128)(4,1)} %broadcast_compare_fusion.4), kind=kOutput, calls=%fused_computation.4.clone.1 | convolution fusion | flops 824180736 | bytes 28835840 | tf_op jit(solution)/shard_map/while/body/eval_jaxpr/hqk,khd->qhd/dot_general | solution.py:113
  357.4 0.9 copy-done.1
  358.9 0.6 fusion.51
  359.6 1.2 broadcast_compare_fusion.4
  360.8 2.1 constant_dynamic-slice_fusion.3
  362.8 1.6 copy.34
  364.5 13.0 %fusion.52 = (f32[12,512]{1,0:T(8,128)S(1)}, f32[12,1024,512]{2,1,0:T(8,128)}) fusion(pred[512,1024]{0,1:T(8,128)(4,1)} %broadcast_compare_fusion.4, bf16[1024,12,64]{0,2,1:T(8,128)(2,1)} %bitcast.67, bf16[512,12,64]{0,2,1:T(8,128)(2,1)} %get-tuple-element.289), kind=kOutput, calls=%fused_computation.2.clone.1 | convolution fusion | flops 824174592 | bytes 28073984 | tf_op jit(solution)/shard_map/while/body/eval_jaxpr/qhd,khd->hqk/dot_general | solution.py:102
  377.4 1.6 copy.33
  379.1 10.9 %fusion.53 = f32[12,64,512]{2,1,0:T(8,128)S(1)} fusion(bf16[1024,12,64]{0,2,1:T(8,128)(2,1)} %bitcast.68, f32[12,1024,512]{2,1,0:T(8,128)} %get-tuple-element.258, pred[512,1024]{0,1:T(8,128)(4,1)} %broadcast_compare_fusion.4), kind=kOutput, calls=%fused_computation.4.clone.1 | convolution fusion | flops 824180736 | bytes 28835840 | tf_op jit(solution)/shard_map/while/body/eval_jaxpr/hqk,khd->qhd/dot_general | solution.py:113
  390.8 0.9 copy-done.1
  392.3 0.6 fusion.51
  392.9 1.2 broadcast_compare_fusion.4
  394.1 2.1 constant_dynamic-slice_fusion.3
  396.2 1.6 copy.34
  397.8 13.0 %fusion.52 = (f32[12,512]{1,0:T(8,128)S(1)}, f32[12,1024,512]{2,1,0:T(8,128)}) fusion(pred[512,1024]{0,1:T(8,128)(4,1)} %broadcast_compare_fusion.4, bf16[1024,12,64]{0,2,1:T(8,128)(2,1)} %bitcast.67, bf16[512,12,64]{0,2,1:T(8,128)(2,1)} %get-tuple-element.289), kind=kOutput, calls=%fused_computation.2.clone.1 | convolution fusion | flops 824174592 | bytes 28073984 | tf_op jit(solution)/shard_map/while/body/eval_jaxpr/qhd,khd->hqk/dot_general | solution.py:102
  410.8 1.6 copy.33
  412.4 10.9 %fusion.53 = f32[12,64,512]{2,1,0:T(8,128)S(1)} fusion(bf16[1024,12,64]{0,2,1:T(8,128)(2,1)} %bitcast.68, f32[12,1024,512]{2,1,0:T(8,128)} %get-tuple-element.258, pred[512,1024]{0,1:T(8,128)(4,1)} %broadcast_compare_fusion.4), kind=kOutput, calls=%fused_computation.4.clone.1 | convolution fusion | flops 824180736 | bytes 28835840 | tf_op jit(solution)/shard_map/while/body/eval_jaxpr/hqk,khd->qhd/dot_general | solution.py:113
  424.1 0.9 copy-done.1
  425.0 2.5 fusion.18
  427.6 0.9 dynamic-slice_reduce_fusion.1
  428.6 62.7 %all-gather.21.cloned.1.call-done = bf16[512,3072]{0,1:T(8,128)(2,1)} async-done(((bf16[512,768]{0,1:T(8,128)(2,1)}), bf16[512,3072]{0,1:T(8,128)(2,1)}) %all-gather.21.cloned.1.call-update) | async-done | bytes 3145744 | tf_op jit(solution)/shard_map/all_gather | solution.py:152
  491.3 6.9 %add_convert_fusion = bf16[512,768]{1,0:T(8,128)(2,1)} fusion(bf16[512,768]{1,0:T(8,128)(2,1)S(1)} %copy-done.7, bf16[512,3072]{0,1:T(8,128)(2,1)} %all-gather.21.cloned.1.call-done, bf16[3072,768]{1,0:T(8,128)(2,1)} %all-gather.23.cloned.1.call-done, f32[768]{0:T(1024)S(1)} %get-tuple-element.157, f32[768]{0:T(1024)S(1)} %get-tuple-element.156, ...), kind=kOutput, calls=%fused_computation.30 | convolution fusion | flops 2417885184 | bytes 9443840 | tf_op jit(solution)/shard_map/dot_general | solution.py:155
  (118 shorter events, 9.6 us)
Async XLA Ops:
  6.5 2.9 copy-start.17
  6.5 2.9 copy-start.21
  6.5 3.0 copy-start.22
  6.5 4.1 copy-start.16
  6.5 68.6 %all-gather.9.cloned.1.call-start = ((), (), s32[]{:S(2)}) async-start(), calls=%async_computation | async-start | bytes 3932160 | tf_op jit(solution)/shard_map/all_gather | solution.py:76
  7.3 107.4 %all-gather.15.cloned.1.call-start = ((), (), s32[]{:S(2)}) async-start(), calls=%async_computation.3 | async-start | bytes 5308416 | tf_op jit(solution)/shard_map/all_gather | solution.py:83
  8.0 147.5 %all-gather.19.cloned.1.call-start = ((), (), s32[]{:S(2)}) async-start(), calls=%async_computation.5 | async-start | bytes 5308416 | tf_op jit(solution)/shard_map/all_gather | solution.py:82
  8.8 187.4 %all-gather.11.cloned.1.call-start = ((), (), s32[]{:S(2)}) async-start(), calls=%async_computation.1 | async-start | bytes 5308416 | tf_op jit(solution)/shard_map/all_gather | solution.py:84
  9.3 234.1 %all-gather.17.cloned.1.call-start = ((), (), s32[]{:S(2)}) async-start(), calls=%async_computation.4 | async-start | bytes 7077888 | tf_op jit(solution)/shard_map/all_gather | solution.py:125
  9.6 194.2 %copy-start.18 = (pred[512]{0:T(512)(128)(4,1)}, pred[512]{0:T(512)(128)(4,1)S(1)}, u32[]{:S(2)}) copy-start(pred[512]{0:T(512)(128)(4,1)S(1)} %subtract_compare_fusion) | copy-start | bytes 1540
  75.1 2.8 copy-start.2
  120.6 1.1 copy-start.3
  161.2 0.6 copy-start.10
  161.5 0.7 copy-start.8
  161.8 0.6 copy-start.13
  161.8 0.6 copy-start.11
  161.9 0.7 copy-start.20
  162.5 0.8 copy-start.14
  162.5 0.9 copy-start.15
  174.9 28.9 %copy-start.9 = (f32[512,12]{0,1:T(8,128)S(1)}, f32[512,12]{0,1:T(8,128)}, u32[]{:S(2)}) copy-start(f32[512,12]{0,1:T(8,128)} %copy-done.8) | copy-start | bytes 73732
  174.9 28.9 %copy-start.12 = (f32[512,12]{0,1:T(8,128)S(1)}, f32[512,12]{0,1:T(8,128)}, u32[]{:S(2)}) copy-start(f32[512,12]{0,1:T(8,128)} %copy-done.11) | copy-start | bytes 73732
  174.9 115.9 %all-gather.13.cloned.1.call-start = ((), (), s32[]{:S(2)}) async-start(), calls=%async_computation.2 | async-start | bytes 7077888 | tf_op jit(solution)/shard_map/all_gather | solution.py:126
  203.0 1.0 copy-start.4
  203.0 225.6 %all-gather.23.cloned.1.call-start = ((), (), s32[]{:S(2)}) async-start(), calls=%async_computation.7 | async-start | bytes 5308416 | tf_op jit(solution)/shard_map/all_gather | solution.py:157
  203.7 287.5 %all-gather.21.cloned.1.call-start = ((), (), s32[]{:S(2)}) async-start(), calls=%async_computation.6 | async-start | bytes 3932160 | tf_op jit(solution)/shard_map/all_gather | solution.py:152
  311.5 11.7 %copy-start = (f32[512,768]{0,1:T(8,128)S(1)}, f32[512,768]{0,1:T(8,128)}, u32[]{:S(2)}) copy-start(f32[512,768]{0,1:T(8,128)} %get-tuple-element.272) | copy-start | bytes 4718596 | tf_op jit(solution)/shard_map/while
  323.2 0.8 copy-start.5
  323.7 1.2 copy-start.1
  324.0 0.9 copy-start.6
  345.7 10.9 %copy-start = (f32[512,768]{0,1:T(8,128)S(1)}, f32[512,768]{0,1:T(8,128)}, u32[]{:S(2)}) copy-start(f32[512,768]{0,1:T(8,128)} %get-tuple-element.272) | copy-start | bytes 4718596 | tf_op jit(solution)/shard_map/while
  356.6 0.8 copy-start.5
  357.1 1.2 copy-start.1
  357.4 0.9 copy-start.6
  379.1 10.9 %copy-start = (f32[512,768]{0,1:T(8,128)S(1)}, f32[512,768]{0,1:T(8,128)}, u32[]{:S(2)}) copy-start(f32[512,768]{0,1:T(8,128)} %get-tuple-element.272) | copy-start | bytes 4718596 | tf_op jit(solution)/shard_map/while
  390.0 0.8 copy-start.5
  390.5 1.2 copy-start.1
  390.8 0.9 copy-start.6
  412.4 10.9 %copy-start = (f32[512,768]{0,1:T(8,128)S(1)}, f32[512,768]{0,1:T(8,128)}, u32[]{:S(2)}) copy-start(f32[512,768]{0,1:T(8,128)} %get-tuple-element.272) | copy-start | bytes 4718596 | tf_op jit(solution)/shard_map/while
  423.3 0.8 copy-start.5
  423.8 1.2 copy-start.1
  424.1 0.9 copy-start.6
  425.0 66.2 %copy-start.7 = (bf16[512,768]{1,0:T(8,128)(2,1)S(1)}, bf16[512,768]{1,0:T(8,128)(2,1)}, u32[]{:S(2)}) copy-start(bf16[512,768]{1,0:T(8,128)(2,1)} %param.12) | copy-start | bytes 2359300
  425.0 66.2 %copy-start.19 = (pred[512]{0:T(512)(128)(4,1)S(1)}, pred[512]{0:T(512)(128)(4,1)}, u32[]{:S(2)}) copy-start(pred[512]{0:T(512)(128)(4,1)} %copy-done.18) | copy-start | bytes 1540
Sparse Core Ops, SparseCore 0:
  8.9 66.1 all-gather.8
  77.0 37.5 all-gather.14
  116.5 38.9 all-gather.18
  157.2 38.9 all-gather.10
  197.9 45.5 all-gather.16
  245.2 45.5 all-gather.12
  292.7 38.9 all-gather.22
  427.7 63.4 all-gather.20
where the time goes:
time: 506 us; the launch traced here: 505 us
  waiting for transfers between devices  303 us (60%)
  matrix products  121 us (24%)
  local copies, waits for them, and re-layouts  38.3 us (8%)
  other arithmetic  28 us (6%)
  between operations  13.9 us (3%)
    all_gather x1, waiting for transfers between devices, shards(): full_rows = lax.all_gather(hidden_states, 'mdl', axis=1, tiled=True)  64.5 us
    all_gather x1, waiting for transfers between devices, shards(): all_heads = lax.all_gather(attended, 'mdl', axis=1, tiled=True)  62.7 us
    dot_general x4, matrix products, block_terms(): jnp.einsum('qhd,khd->hqk', query, block_keys.reshape(size, local_heads, h...  51.9 us
    all_gather x1, waiting for transfers between devices, shards(): values_piece = lax.all_gather(value_flat, 'tok', axis=0, tiled=True)  47.3 us
    dot_general x4, matrix products, block_terms(): jnp.einsum('hqk,khd->qhd', expo.astype(jnp.bfloat16), block_values.reshap...  44.4 us
    all_gather x1, waiting for transfers between devices, shards(): keys_piece = lax.all_gather(key_flat, 'tok', axis=0, tiled=True)  38.2 us
    all_gather x1, waiting for transfers between devices, shards(): lax.all_gather(query_weight, 'tok', axis=0, tiled=True)  33.6 us
    all_gather x1, waiting for transfers between devices, shards(): lax.all_gather(key_weight, 'tok', axis=0, tiled=True)  32 us
  transfers between devices with their start and end apart: 8, of which 7 were waited for; matrix products, arithmetic and copies ran while one was open for 34% of the time, Pallas kernels for 0%

commit v1 on v0

--- a/solution.py
+++ b/solution.py
@@ -73,7 +73,15 @@
     local_width = query_weight.shape[1]
     head_width = query_gain.shape[0]
     local_heads = local_width // head_width
-    full_rows = lax.all_gather(hidden_states, "mdl", axis=1, tiled=True)
+    ways, here = (lax.axis_size("mdl"), lax.axis_index("mdl"))
+    grown, reach = (hidden_states, 1)
+    while reach < ways:
+        theirs = lax.ppermute(grown, "mdl", [(d, d ^ reach) for d in range(ways)])
+        mine_first = jnp.concatenate([grown, theirs], axis=1)
+        theirs_first = jnp.concatenate([theirs, grown], axis=1)
+        grown = jnp.where(here & reach == 0, mine_first, theirs_first)
+        reach = 2 * reach
+    full_rows = grown
     row_index = lax.axis_index("tok") * own_rows + jnp.arange(own_rows, dtype=jnp.int32)
     request, is_text, bound = token_labels(row_index, lengths)
     normed = modulate(full_rows, modulation, is_text)

time: 506 us -> 443 us (0.88)
  waiting for transfers between devices: 303 us -> 233 us
  starting transfers between devices: 0.49 us -> 6.35 us
    ppermute x0 -> x2, waiting for transfers between devices: none -> 84 us  [shards(): theirs = lax.ppermute(grown, 'mdl', [(d, d ^ reach) for d in range(ways)])]
    all_gather x1 -> x0, waiting for transfers between devices: 64.5 us -> none  [shards(): full_rows = lax.all_gather(hidden_states, 'mdl', axis=1, tiled=True)]
    all_gather x1, waiting for transfers between devices: 33.6 us -> 0.01 us  [shards(): lax.all_gather(query_weight, 'tok', axis=0, tiled=True)]
    all_gather x1, waiting for transfers between devices: 32 us -> 0.01 us  [shards(): lax.all_gather(key_weight, 'tok', axis=0, tiled=True)]
    all_gather x1, waiting for transfers between devices: 21 us -> 0.02 us  [shards(): lax.all_gather(value_weight, 'tok', axis=0, tiled=True)]
    ppermute x0 -> x2, starting transfers between devices: none -> 5.9 us  [shards(): theirs = lax.ppermute(grown, 'mdl', [(d, d ^ reach) for d in range(ways)])]
  transfers between devices with their start and end apart: 8 -> 9, of which waited for: 7 -> 5; matrix products, arithmetic and copies ran while one was open for 34% -> 40% of each run, Pallas kernels for 0% -> 0%
where the time goes in v1:
time: 443 us; the launch traced here: 442 us
  waiting for transfers between devices  233 us (53%)
  matrix products  122 us (28%)
  local copies, waits for them, and re-layouts  36.9 us (8%)
  other arithmetic  29.5 us (7%)
  between operations  13.9 us (3%)
  starting transfers between devices  6.35 us (1%)
    ppermute x2, waiting for transfers between devices, shards(): theirs = lax.ppermute(grown, 'mdl', [(d, d ^ reach) for d in range(ways)])  84 us
    all_gather x1, waiting for transfers between devices, shards(): all_heads = lax.all_gather(attended, 'mdl', axis=1, tiled=True)  62.7 us
    dot_general x4, matrix products, block_terms(): jnp.einsum('qhd,khd->hqk', query, block_keys.reshape(size, local_heads, h...  51.9 us
    all_gather x1, waiting for transfers between devices, shards(): values_piece = lax.all_gather(value_flat, 'tok', axis=0, tiled=True)  47.3 us
    dot_general x4, matrix products, block_terms(): jnp.einsum('hqk,khd->qhd', expo.astype(jnp.bfloat16), block_values.reshap...  44.4 us
    all_gather x1, waiting for transfers between devices, shards(): keys_piece = lax.all_gather(key_flat, 'tok', axis=0, tiled=True)  37.4 us
    dynamic_slice x16, local copies, waits for them, and re-layouts, shards(): lax.scan(step_block, initial, (keys_piece.reshape(steps_count, block, loc...  23.7 us
    dot_general x3, matrix products, shards(): jnp.dot(columns, pieces[number], preferred_element_type=jnp.float32)  18.9 us
  transfers between devices with their start and end apart: 9, of which 5 were waited for; matrix products, arithmetic and copies ran while one was open for 40% of the time, Pallas kernels for 0%

profile of v1, /device:TPU:0, one launch (start us, length us, event | category | flops | bytes accessed | tf_op | source)
XLA Modules:
  0.0 442.4 jit_solution(3644226987056116571)
XLA Ops:
  6.6 0.7 all-gather.12.cloned.1.call-update
  7.3 0.7 all-gather.16.cloned.1.call-update
  8.1 3.1 collective-permute-start
  11.2 17.7 %collective-permute-done = bf16[512,768]{1,0:T(8,128)(2,1)S(1)} collective-permute-done((bf16[512,768]{1,0:T(8,128)(2,1)}, bf16[512,768]{1,0:T(8,128)(2,1)S(1)}, u32[]{:S(2)}, u32[]{:S(2)}) %collective-permute-start) | collective-permute-done | bytes 786464 | tf_op jit(solution)/shard_map/ppermute | solution.py:79
  28.9 1.8 maximum_select_fusion.1
  30.8 2.8 collective-permute-start.1
  33.8 1.0 fusion.20
  34.8 66.3 %collective-permute-done.1 = bf16[512,1536]{1,0:T(8,128)(2,1)S(1)} collective-permute-done((bf16[512,1536]{1,0:T(8,128)(2,1)S(1)}, bf16[512,1536]{1,0:T(8,128)(2,1)S(1)}, u32[]{:S(2)}, u32[]{:S(2)}) %collective-permute-start.1) | collective-permute-done | bytes 1572896 | tf_op jit(solution)/shard_map/ppermute | solution.py:79
  101.1 1.0 convert_reduce_fusion
  102.1 1.6 fusion.13
  103.7 4.1 fusion.16
  107.9 5.9 %fusion.25 = f32[512,768]{1,0:T(8,128)S(1)} fusion(bf16[512,3072]{1,0:T(8,128)(2,1)} %fusion.16, bf16[3072,768]{1,0:T(8,128)(2,1)} %all-gather.12.cloned.1.call-done), kind=kOutput, calls=%fused_computation.66 | convolution fusion | flops 2415919104 | bytes 9437184 | tf_op jit(solution)/shard_map/dot_general | solution.py:97
  114.9 6.3 %fusion.26 = f32[512,768]{0,1:T(8,128)S(1)} fusion(bf16[512,3072]{1,0:T(8,128)(2,1)} %fusion.16, bf16[3072,768]{1,0:T(8,128)(2,1)} %all-gather.16.cloned.1.call-done), kind=kOutput, calls=%fused_computation.67 | convolution fusion | flops 2415919104 | bytes 9437184 | tf_op jit(solution)/shard_map/dot_general | solution.py:97
  122.9 1.3 multiply_subtract_fusion
  124.3 1.2 copy.23
  125.5 0.9 mul.163
  126.4 1.6 copy.22
  128.1 0.9 sub.56
  129.0 1.6 copy.21
  130.7 3.9 select_convert_fusion
  134.8 6.8 %convolution_convert_fusion = bf16[512,768]{1,0:T(8,128)(2,1)} fusion(bf16[512,3072]{1,0:T(8,128)(2,1)} %fusion.16, bf16[3072,768]{1,0:T(8,128)(2,1)} %all-gather.8.cloned.1.call-done), kind=kOutput, calls=%fused_computation.38 | convolution fusion | flops 2416312320 | bytes 8650752 | tf_op jit(solution)/shard_map/dot_general | solution.py:97
  142.3 1.3 fusion.17
  143.7 37.4 %all-gather.14.cloned.1.call-done = bf16[4096,768]{1,0:T(8,128)(2,1)} async-done(((bf16[512,768]{1,0:T(8,128)(2,1)}), bf16[4096,768]{1,0:T(8,128)(2,1)}) %all-gather.14.cloned.1.call-update) | async-done | bytes 6291472 | tf_op jit(solution)/shard_map/all_gather | solution.py:133
  181.0 47.3 %all-gather.10.cloned.1.call-done = bf16[4096,768]{1,0:T(8,128)(2,1)} async-done(((bf16[512,768]{1,0:T(8,128)(2,1)}), bf16[4096,768]{1,0:T(8,128)(2,1)}) %all-gather.10.cloned.1.call-update) | async-done | bytes 6291472 | tf_op jit(solution)/shard_map/all_gather | solution.py:134
  228.3 134.2 %while.15 = (s32[]{:T(128)}, f32[512,768]{0,1:T(8,128)}, f32[512,12]{0,1:T(8,128)}, bf16[4,1024,768]{2,1,0:T(8,128)(2,1)}, s32[4]{0:T(128)S(1)}, /*index=5*/s32[...) while((s32[]{:T(128)}, f32[512,768]{0,1:T(8,128)}, ...), condition=%wide.region_8.9_spmd.clone.clone.clone, body=%wide.region_6.8_spmd.clone.clone.clone.sunk | while | flops 1649682944 | bytes 87601416 | solution.py:145
  228.9 0.6 fusion.51
  229.6 1.2 broadcast_compare_fusion.4
  230.7 2.1 constant_dynamic-slice_fusion.3
  232.8 1.6 copy.34
  234.4 13.0 %fusion.52 = (f32[12,512]{1,0:T(8,128)S(1)}, f32[12,1024,512]{2,1,0:T(8,128)}) fusion(pred[512,1024]{0,1:T(8,128)(4,1)} %broadcast_compare_fusion.4, bf16[1024,12,64]{0,2,1:T(8,128)(2,1)} %bitcast.67, bf16[512,12,64]{0,2,1:T(8,128)(2,1)} %get-tuple-element.289), kind=kOutput, calls=%fused_computation.2.clone.1 | convolution fusion | flops 824174592 | bytes 28073984 | tf_op jit(solution)/shard_map/while/body/eval_jaxpr/qhd,khd->hqk/dot_general | solution.py:110
  247.4 1.6 copy.33
  249.0 11.7 %fusion.53 = f32[12,64,512]{2,1,0:T(8,128)S(1)} fusion(bf16[1024,12,64]{0,2,1:T(8,128)(2,1)} %bitcast.68, f32[12,1024,512]{2,1,0:T(8,128)} %get-tuple-element.258, pred[512,1024]{0,1:T(8,128)(4,1)} %broadcast_compare_fusion.4), kind=kOutput, calls=%fused_computation.4.clone.1 | convolution fusion | flops 824180736 | bytes 28835840 | tf_op jit(solution)/shard_map/while/body/eval_jaxpr/hqk,khd->qhd/dot_general | solution.py:121
  261.5 0.9 copy-done.1
  262.4 0.6 dynamic_slice.29
  263.0 0.6 fusion.51
  263.7 1.2 broadcast_compare_fusion.4
  264.9 2.1 constant_dynamic-slice_fusion.3
  266.9 1.6 copy.34
  268.6 13.0 %fusion.52 = (f32[12,512]{1,0:T(8,128)S(1)}, f32[12,1024,512]{2,1,0:T(8,128)}) fusion(pred[512,1024]{0,1:T(8,128)(4,1)} %broadcast_compare_fusion.4, bf16[1024,12,64]{0,2,1:T(8,128)(2,1)} %bitcast.67, bf16[512,12,64]{0,2,1:T(8,128)(2,1)} %get-tuple-element.289), kind=kOutput, calls=%fused_computation.2.clone.1 | convolution fusion | flops 824174592 | bytes 28073984 | tf_op jit(solution)/shard_map/while/body/eval_jaxpr/qhd,khd->hqk/dot_general | solution.py:110
  281.6 1.6 copy.33
  283.2 10.9 %fusion.53 = f32[12,64,512]{2,1,0:T(8,128)S(1)} fusion(bf16[1024,12,64]{0,2,1:T(8,128)(2,1)} %bitcast.68, f32[12,1024,512]{2,1,0:T(8,128)} %get-tuple-element.258, pred[512,1024]{0,1:T(8,128)(4,1)} %broadcast_compare_fusion.4), kind=kOutput, calls=%fused_computation.4.clone.1 | convolution fusion | flops 824180736 | bytes 28835840 | tf_op jit(solution)/shard_map/while/body/eval_jaxpr/hqk,khd->qhd/dot_general | solution.py:121
  294.9 0.9 copy-done.1
  295.8 0.6 dynamic_slice.29
  296.4 0.6 fusion.51
  297.0 1.2 broadcast_compare_fusion.4
  298.2 2.1 constant_dynamic-slice_fusion.3
  300.3 1.6 copy.34
  301.9 13.0 %fusion.52 = (f32[12,512]{1,0:T(8,128)S(1)}, f32[12,1024,512]{2,1,0:T(8,128)}) fusion(pred[512,1024]{0,1:T(8,128)(4,1)} %broadcast_compare_fusion.4, bf16[1024,12,64]{0,2,1:T(8,128)(2,1)} %bitcast.67, bf16[512,12,64]{0,2,1:T(8,128)(2,1)} %get-tuple-element.289), kind=kOutput, calls=%fused_computation.2.clone.1 | convolution fusion | flops 824174592 | bytes 28073984 | tf_op jit(solution)/shard_map/while/body/eval_jaxpr/qhd,khd->hqk/dot_general | solution.py:110
  314.9 1.6 copy.33
  316.5 10.9 %fusion.53 = f32[12,64,512]{2,1,0:T(8,128)S(1)} fusion(bf16[1024,12,64]{0,2,1:T(8,128)(2,1)} %bitcast.68, f32[12,1024,512]{2,1,0:T(8,128)} %get-tuple-element.258, pred[512,1024]{0,1:T(8,128)(4,1)} %broadcast_compare_fusion.4), kind=kOutput, calls=%fused_computation.4.clone.1 | convolution fusion | flops 824180736 | bytes 28835840 | tf_op jit(solution)/shard_map/while/body/eval_jaxpr/hqk,khd->qhd/dot_general | solution.py:121
  328.2 0.9 copy-done.1
  329.1 0.6 dynamic_slice.29
  329.7 0.6 fusion.51
  330.4 1.2 broadcast_compare_fusion.4
  331.5 2.1 constant_dynamic-slice_fusion.3
  333.6 1.6 copy.34
  335.3 13.0 %fusion.52 = (f32[12,512]{1,0:T(8,128)S(1)}, f32[12,1024,512]{2,1,0:T(8,128)}) fusion(pred[512,1024]{0,1:T(8,128)(4,1)} %broadcast_compare_fusion.4, bf16[1024,12,64]{0,2,1:T(8,128)(2,1)} %bitcast.67, bf16[512,12,64]{0,2,1:T(8,128)(2,1)} %get-tuple-element.289), kind=kOutput, calls=%fused_computation.2.clone.1 | convolution fusion | flops 824174592 | bytes 28073984 | tf_op jit(solution)/shard_map/while/body/eval_jaxpr/qhd,khd->hqk/dot_general | solution.py:110
  348.2 1.6 copy.33
  349.9 10.9 %fusion.53 = f32[12,64,512]{2,1,0:T(8,128)S(1)} fusion(bf16[1024,12,64]{0,2,1:T(8,128)(2,1)} %bitcast.68, f32[12,1024,512]{2,1,0:T(8,128)} %get-tuple-element.258, pred[512,1024]{0,1:T(8,128)(4,1)} %broadcast_compare_fusion.4), kind=kOutput, calls=%fused_computation.4.clone.1 | convolution fusion | flops 824180736 | bytes 28835840 | tf_op jit(solution)/shard_map/while/body/eval_jaxpr/hqk,khd->qhd/dot_general | solution.py:121
  361.5 0.9 copy-done.1
  362.5 2.5 fusion.18
  365.0 0.9 dynamic-slice_reduce_fusion.1
  366.0 62.7 %all-gather.18.cloned.1.call-done = bf16[512,3072]{0,1:T(8,128)(2,1)} async-done(((bf16[512,768]{0,1:T(8,128)(2,1)}), bf16[512,3072]{0,1:T(8,128)(2,1)}) %all-gather.18.cloned.1.call-update) | async-done | bytes 3145744 | tf_op jit(solution)/shard_map/all_gather | solution.py:160
  428.7 6.9 %add_convert_fusion = bf16[512,768]{1,0:T(8,128)(2,1)} fusion(bf16[512,768]{1,0:T(8,128)(2,1)S(1)} %copy-done.6, bf16[512,3072]{0,1:T(8,128)(2,1)} %all-gather.18.cloned.1.call-done, bf16[3072,768]{1,0:T(8,128)(2,1)} %all-gather.20.cloned.1.call-done, f32[768]{0:T(1024)S(1)} %get-tuple-element.157, f32[768]{0:T(1024)S(1)} %get-tuple-element.156, ...), kind=kOutput, calls=%fused_computation.32 | convolution fusion | flops 2417885184 | bytes 9443840 | tf_op jit(solution)/shard_map/dot_general | solution.py:163
  (118 shorter events, 7.6 us)
Async XLA Ops:
  6.5 27.0 %copy-start.16 = (s32[3,512]{1,0:T(4,128)S(1)}, s32[3,512]{1,0:T(4,128)}, u32[]{:S(2)}) copy-start(s32[3,512]{1,0:T(4,128)} %param.14) | copy-start | bytes 18436
  6.5 27.0 %copy-start.20 = (f32[64]{0:T(128)S(1)}, f32[64]{0:T(128)}, u32[]{:S(2)}) copy-start(f32[64]{0:T(128)} %param.21) | copy-start | bytes 772
  6.5 27.1 %copy-start.21 = (s32[2]{0:T(128)S(1)}, s32[2]{0:T(128)}, u32[]{:S(2)}) copy-start(s32[2]{0:T(128)} %param.13) | copy-start | bytes 28
  6.5 28.2 %copy-start.15 = (f32[6,3072]{1,0:T(8,128)S(1)}, f32[6,3072]{1,0:T(8,128)}, u32[]{:S(2)}) copy-start(f32[6,3072]{1,0:T(8,128)} %param.15) | copy-start | bytes 221188
  6.5 101.3 %all-gather.12.cloned.1.call-start = ((), (), s32[]{:S(2)}) async-start(), calls=%async_computation.2 | async-start | bytes 5308416 | tf_op jit(solution)/shard_map/all_gather | solution.py:91
  7.3 107.6 %all-gather.16.cloned.1.call-start = ((), (), s32[]{:S(2)}) async-start(), calls=%async_computation.4 | async-start | bytes 5308416 | tf_op jit(solution)/shard_map/all_gather | solution.py:90
  8.0 126.8 %all-gather.8.cloned.1.call-start = ((), (), s32[]{:S(2)}) async-start(), calls=%async_computation | async-start | bytes 5308416 | tf_op jit(solution)/shard_map/all_gather | solution.py:92
  8.1 20.8 %collective-permute-start = (bf16[512,768]{1,0:T(8,128)(2,1)}, bf16[512,768]{1,0:T(8,128)(2,1)S(1)}, u32[]{:S(2)}, u32[]{:S(2)}) collective-permute-start(bf16[512,768]{1,0:T(8,128)(2,1)} %param.12), channel_id=1, source_target_pairs={{0,1},{1,0},{2,3},{3,2},{4,5},{5,4},{6,7},{7,6},{8,9},{9,8},{10,11... | collective-permute-start | bytes 2359304 | tf_op jit(solution)/shard_map/ppermute | solution.py:79
  11.2 169.8 %all-gather.14.cloned.1.call-start = ((), (), s32[]{:S(2)}) async-start(), calls=%async_computation.3 | async-start | bytes 7077888 | tf_op jit(solution)/shard_map/all_gather | solution.py:133
  30.8 70.4 %collective-permute-start.1 = (bf16[512,1536]{1,0:T(8,128)(2,1)S(1)}, bf16[512,1536]{1,0:T(8,128)(2,1)S(1)}, u32[]{:S(2)}, u32[]{:S(2)}) collective-permute-start(bf16[512,1536]{1,0:T(8,128)(2,1)S(1)} %maximum_select_fusion.1), channel_id=1, source_target_pairs={{0,2},{1,3},{2,0},{3,1},{4,6},{5,7},{6,4},{7,5},{8,10},{9,11},{10,... | collective-permute-start | bytes 4718600 | tf_op jit(solution)/shard_map/ppermute | solution.py:79
  33.7 108.5 %copy-start.17 = (pred[512]{0:T(512)(128)(4,1)}, pred[512]{0:T(512)(128)(4,1)S(1)}, u32[]{:S(2)}) copy-start(pred[512]{0:T(512)(128)(4,1)S(1)} %subtract_compare_fusion) | copy-start | bytes 1540
  113.8 1.1 copy-start.2
  121.4 1.0 copy-start.9
  121.4 1.0 copy-start.19
  121.7 1.1 copy-start.7
  122.0 0.8 copy-start.12
  122.0 0.8 copy-start.10
  122.0 0.9 copy-start.13
  122.1 0.9 copy-start.14
  134.6 7.8 %copy-start.3 = (bf16[512,12,32]{0,2,1:T(8,128)(2,1)S(1)}, bf16[512,12,32]{0,2,1:T(8,128)(2,1)}, u32[]{:S(2)}) copy-start(bf16[512,12,32]{0,2,1:T(8,128)(2,1)} %get-tuple-element.181) | copy-start | bytes 1179652
  134.6 7.8 %copy-start.8 = (f32[512,12]{0,1:T(8,128)S(1)}, f32[512,12]{0,1:T(8,128)}, u32[]{:S(2)}) copy-start(f32[512,12]{0,1:T(8,128)} %copy-done.7) | copy-start | bytes 73732
  134.6 7.8 %copy-start.11 = (f32[512,12]{0,1:T(8,128)S(1)}, f32[512,12]{0,1:T(8,128)}, u32[]{:S(2)}) copy-start(f32[512,12]{0,1:T(8,128)} %copy-done.10) | copy-start | bytes 73732
  134.6 93.7 %all-gather.10.cloned.1.call-start = ((), (), s32[]{:S(2)}) async-start(), calls=%async_computation.1 | async-start | bytes 7077888 | tf_op jit(solution)/shard_map/all_gather | solution.py:134
  141.6 224.3 %all-gather.20.cloned.1.call-start = ((), (), s32[]{:S(2)}) async-start(), calls=%async_computation.6 | async-start | bytes 5308416 | tf_op jit(solution)/shard_map/all_gather | solution.py:165
  142.2 286.5 %all-gather.18.cloned.1.call-start = ((), (), s32[]{:S(2)}) async-start(), calls=%async_computation.5 | async-start | bytes 3932160 | tf_op jit(solution)/shard_map/all_gather | solution.py:160
  249.0 11.7 %copy-start = (f32[512,768]{0,1:T(8,128)S(1)}, f32[512,768]{0,1:T(8,128)}, u32[]{:S(2)}) copy-start(f32[512,768]{0,1:T(8,128)} %get-tuple-element.272) | copy-start | bytes 4718596 | tf_op jit(solution)/shard_map/while
  260.7 0.8 copy-start.4
  261.2 1.2 copy-start.1
  261.5 0.9 copy-start.5
  283.2 10.9 %copy-start = (f32[512,768]{0,1:T(8,128)S(1)}, f32[512,768]{0,1:T(8,128)}, u32[]{:S(2)}) copy-start(f32[512,768]{0,1:T(8,128)} %get-tuple-element.272) | copy-start | bytes 4718596 | tf_op jit(solution)/shard_map/while
  294.1 0.8 copy-start.4
  294.6 1.2 copy-start.1
  294.8 0.9 copy-start.5
  316.5 10.9 %copy-start = (f32[512,768]{0,1:T(8,128)S(1)}, f32[512,768]{0,1:T(8,128)}, u32[]{:S(2)}) copy-start(f32[512,768]{0,1:T(8,128)} %get-tuple-element.272) | copy-start | bytes 4718596 | tf_op jit(solution)/shard_map/while
  327.4 0.8 copy-start.4
  327.9 1.2 copy-start.1
  328.2 0.9 copy-start.5
  349.9 10.9 %copy-start = (f32[512,768]{0,1:T(8,128)S(1)}, f32[512,768]{0,1:T(8,128)}, u32[]{:S(2)}) copy-start(f32[512,768]{0,1:T(8,128)} %get-tuple-element.272) | copy-start | bytes 4718596 | tf_op jit(solution)/shard_map/while
  360.8 0.8 copy-start.4
  361.3 1.2 copy-start.1
  361.5 0.9 copy-start.5
  362.5 66.2 %copy-start.6 = (bf16[512,768]{1,0:T(8,128)(2,1)S(1)}, bf16[512,768]{1,0:T(8,128)(2,1)}, u32[]{:S(2)}) copy-start(bf16[512,768]{1,0:T(8,128)(2,1)} %param.12) | copy-start | bytes 2359300
  362.5 66.2 %copy-start.18 = (pred[512]{0:T(512)(128)(4,1)S(1)}, pred[512]{0:T(512)(128)(4,1)}, u32[]{:S(2)}) copy-start(pred[512]{0:T(512)(128)(4,1)} %copy-done.17) | copy-start | bytes 1540
Sparse Core Ops, SparseCore 0:
  9.3 41.6 all-gather.11
  52.8 38.9 all-gather.15
  93.6 38.9 all-gather.7
  134.7 46.2 all-gather.13
  182.7 45.5 all-gather.9
  230.0 38.9 all-gather.19
  365.1 63.4 all-gather.17
